TPU v7x, 32 devices: a whole 2x2x4 slice. The times are simulated.
32 devices in a mesh: seq: 8 (over z, x), head: 4 (over y, core).
Axes of the slice: x: 2, y: 2, z: 4, core: 2. Of those that a mesh axis runs over, the one named last changes fastest.
Arguments:
- hidden: bfloat16 [8192, 8192], P('seq'), may hold values from -27 to 27, as said below
- key_value_weight: bfloat16 [8192, 2048], P('seq', 'head'), may hold values from -0.0625 to 0.0625
- down_projection: bfloat16 [2048, 512], P('head'), may hold values from -0.125 to 0.125
- up_projection: bfloat16 [512, 2048], P(None, 'head'), may hold values from -0.25 to 0.25
- positions: int32 [8192], P('seq'), may hold values from 0 to 131071
Outputs:
- grad_down: float32 [512, 2048], P('seq', 'head')
- grad_up: float32 [512, 2048], P('seq', 'head')
- rel_error: float32 [], replicated
Inputs may be any that keep to these rules, and one draw needn't show every extreme that they name: `hidden`: real-valued inputs, rows of differing scale.
All inputs are finite; a program needn't handle non-finite values.
Results may differ from a plain program's by a relative error of at most 0.0045.
Values may be sent and summed in bfloat16 or wider, within the bound.
A program may use at most 64 MiB of HBM per device.

v0:
```python
import math

import jax
import jax.numpy as jnp
from jax import lax
from jax.sharding import PartitionSpec as P

KEY_VALUE_HEADS = 8
HEAD_SIZE = 128


THETA = 500000.0


def rotate_targets(dense, positions):
    half_dim = HEAD_SIZE // 2
    freqs = jnp.power(
        jnp.float32(THETA), -(jnp.arange(half_dim, dtype=jnp.float32) * 2.0 / HEAD_SIZE)
    )
    angle = positions.astype(jnp.float32)[:, None] * freqs[None, :]
    cosine = jnp.cos(angle)[:, None, :]
    sine = jnp.sin(angle)[:, None, :]
    shaped = dense.reshape(dense.shape[0], -1, 2, HEAD_SIZE)
    key_part = shaped[:, :, 0, :]
    first = key_part[..., :half_dim]
    second = key_part[..., half_dim:]
    turned = jnp.concatenate(
        [first * cosine - second * sine, second * cosine + first * sine], axis=-1
    )
    joined = jnp.stack([turned, shaped[:, :, 1, :]], axis=2)
    return joined.reshape(dense.shape[0], -1).astype(jnp.bfloat16)


def per_device(hidden, key_value_weight, down_projection, up_projection, positions):
    rows_here = hidden.shape[0]
    total_row_count = lax.axis_size("seq") * rows_here
    entry_items = total_row_count * 2 * KEY_VALUE_HEADS * HEAD_SIZE
    dense = jnp.dot(
        hidden,
        lax.all_gather(key_value_weight, "seq", axis=0, tiled=True),
        preferred_element_type=jnp.float32,
    )
    targets = rotate_targets(dense, positions)
    target_wide = targets.astype(jnp.float32)
    energy_local = jnp.sum(target_wide * target_wide)
    partial_value = jnp.dot(targets, down_projection, preferred_element_type=jnp.float32)
    latent = lax.psum(partial_value, "head").astype(jnp.bfloat16)
    rebuilt = jnp.dot(latent, up_projection, preferred_element_type=jnp.float32)
    residual = target_wide - rebuilt
    misfit_local = jnp.sum(residual * residual)
    latent_wide = latent.astype(jnp.float32)
    up_wide = up_projection.astype(jnp.float32)
    grad_up = lax.dot_general(
        latent_wide,
        residual,
        (((0,), (0,)), ((), ())),
        precision=lax.Precision.HIGHEST,
        preferred_element_type=jnp.float32,
    )
    local_grad = lax.dot_general(
        residual,
        up_wide,
        (((1,), (1,)), ((), ())),
        precision=lax.Precision.HIGHEST,
        preferred_element_type=jnp.float32,
    )
    d_latent = lax.psum(local_grad, "head").astype(jnp.bfloat16)
    grad_down = lax.dot_general(
        d_latent, targets, (((0,), (0,)), ((), ())), preferred_element_type=jnp.float32
    )
    grad_down, grad_up = (
        lax.psum_scatter(grad_down, "seq", scatter_dimension=0, tiled=True),
        lax.psum_scatter(grad_up, "seq", scatter_dimension=0, tiled=True),
    )
    misfit, energy = lax.psum((misfit_local, energy_local), ("seq", "head"))
    rel_error = misfit / energy
    factor = -(entry_items / energy) / math.sqrt(total_row_count)
    grad_down = factor * grad_down
    grad_up = factor * grad_up
    return (grad_down, grad_up, rel_error)


def solution(mesh):
    return jax.shard_map(
        per_device,
        mesh=mesh,
        in_specs=(P("seq", None), P("seq", "head"), P("head", None), P(None, "head"), P("seq")),
        out_specs=(P("seq", "head"), P("seq", "head"), P()),
        check_vma=False,
    )
```

profile of v0, /device:TPU:8, one launch (start us, length us, event | category | flops | bytes accessed | tf_op | source)
XLA Modules:
  0.0 347.8 jit_solution(8485636736758103250)
XLA Ops:
  7.2 0.0 copy-start
  7.2 0.0 all-gather.2.cloned.1.call-start
  7.2 0.7 all-gather.2.cloned.1.call-update
  7.9 0.0 reduce-scatter.5.cloned.1.call-start
  8.0 0.7 convert_element_type.24
  8.7 1.0 multiply_cosine_fusion
  9.7 124.3 %all-gather.2.cloned.1.call-done = bf16[8192,512]{1,0:T(8,128)(2,1)} async-done(((bf16[1024,512]{1,0:T(8,128)(2,1)}), bf16[8192,512]{1,0:T(8,128)(2,1)}) %all-gather.2.cloned.1.call-update) | async-done | bytes 8388624 | tf_op jit(solution)/shard_map/all_gather | solution.py:40
  133.9 17.2 %fusion.5 = f32[1024,512]{0,1:T(8,128)S(1)} fusion(bf16[1024,8192]{1,0:T(8,128)(2,1)} %param.5, bf16[8192,512]{1,0:T(8,128)(2,1)} %all-gather.2.cloned.1.call-done), kind=kOutput, calls=%fused_computation.18 | convolution fusion | flops 8589934592 | bytes 27262976 | tf_op jit(solution)/shard_map/dot_general | solution.py:38
  151.2 0.1 slice.19
  151.3 0.1 slice_bitcast_fusion
  151.4 0.2 multiply_subtract_fusion
  151.6 0.0 copy-start.4
  151.6 1.1 multiply_reduce_fusion.1
  152.7 0.0 copy-start.1
  152.7 1.3 copy.10
  154.1 0.0 copy-done.4
  154.1 2.1 fusion.6
  156.2 0.0 copy-done.1
  156.2 41.2 %all-reduce.3 = bf16[1024,512]{1,0:T(8,128)(2,1)} all-reduce(f32[1024,512]{1,0:T(8,128)} %fusion.6), channel_id=1, replica_groups=mesh['seq'=8,'head'=4] {'head'}, use_global_device_ids=true, to_apply=%region_2.0 | all-reduce | flops 524288 | bytes 3145728 | tf_op jit(solution)/shard_map/psum | solution.py:47
  197.3 0.0 copy-done
  197.3 0.0 copy-start.3
  197.4 3.2 multiply_reduce_fusion
  200.6 0.0 copy-done.3
  200.6 2.9 fusion.9
  203.5 3.2 fusion.7
  206.7 0.0 copy-start.2
  206.7 0.0 reduce-scatter.5.cloned.1.call-update
  206.7 0.0 reduce-scatter.3.cloned.1.call-start
  206.7 43.3 %all-reduce.4 = bf16[1024,512]{1,0:T(8,128)(2,1)S(1)} all-reduce(f32[1024,512]{1,0:T(8,128)} %fusion.7), channel_id=1, replica_groups=mesh['seq'=8,'head'=4] {'head'}, use_global_device_ids=true, to_apply=%region_3.0 | all-reduce | flops 524288 | bytes 3145728 | tf_op jit(solution)/shard_map/psum | solution.py:67
  250.1 0.0 copy-done.2
  250.1 1.7 fusion.8
  251.8 0.0 reduce-scatter.3.cloned.1.call-update
  251.9 39.8 %all-reduce = (f32[]{:T(128)}, f32[]{:T(128)}) all-reduce(f32[]{:T(128)} %get-tuple-element.5, f32[]{:T(128)} %get-tuple-element.11), channel_id=1, replica_groups=mesh['seq'=8,'head'=4] {'seq','head'}, use_global_device_ids=true, to_apply=%region_1.0 | all-reduce | flops 2 | bytes 16 | tf_op jit(solution)/shard_map/psum | solution.py:75
  293.7 0.0 reduce-scatter.5.cloned.1.call-done
  293.7 1.6 broadcast_multiply_fusion
  295.3 43.3 %reduce-scatter.3.cloned.1.call-done = f32[64,512]{1,0:T(8,128)} async-done(((f32[512,512]{1,0:T(8,128)}), f32[64,512]{1,0:T(8,128)}) %reduce-scatter.3.cloned.1.call-update) | async-done | bytes 131088 | tf_op jit(solution)/shard_map/reduce_scatter | solution.py:72
  338.6 1.6 broadcast_multiply_fusion.1
  (2 shorter events, 0.0 us)
Async XLA Ops:
  7.2 190.2 %copy-start = (bf16[512,512]{1,0:T(8,128)(2,1)S(1)}, bf16[512,512]{1,0:T(8,128)(2,1)}, u32[]{:S(2)}) copy-start(bf16[512,512]{1,0:T(8,128)(2,1)} %param.8) | copy-start | bytes 1572868
  7.2 126.8 %all-gather.2.cloned.1.call-start = ((), (), s32[]{:S(2)}) async-start(), calls=%async_computation.2 | async-start | bytes 9437184 | tf_op jit(solution)/shard_map/all_gather | solution.py:40
  7.9 285.8 %reduce-scatter.5.cloned.1.call-start = ((), (), s32[]{:S(2)}) async-start(), calls=%async_computation.4 | async-start | bytes 1179648 | tf_op jit(solution)/shard_map/reduce_scatter | solution.py:73
  151.6 2.5 copy-start.4
  152.7 3.4 copy-start.1
  197.3 3.2 copy-start.3
  206.7 43.4 %copy-start.2 = (bf16[1024,2,2,128]{0,3,2,1:T(8,128)(2,1)S(1)}, bf16[1024,2,2,128]{0,3,2,1:T(8,128)(2,1)}, u32[]{:S(2)}) copy-start(bf16[1024,2,2,128]{0,3,2,1:T(8,128)(2,1)} %copy-done.1) | copy-start | bytes 3145732
  206.7 131.9 %reduce-scatter.3.cloned.1.call-start = ((), (), s32[]{:S(2)}) async-start(), calls=%async_computation.3 | async-start | bytes 1179648 | tf_op jit(solution)/shard_map/reduce_scatter | solution.py:72
Sparse Core Ops, SparseCore 0:
  10.1 123.7 all-gather.1
  206.8 64.5 reduce-scatter.4
  274.9 63.7 reduce-scatter.2
where the time goes:
time: 350 us; the launch traced here: 348 us
  waiting for transfers between devices  168 us (48%)
  blocking collectives  124 us (35%)
  matrix products  30.4 us (9%)
  between operations  17 us (5%)
  other arithmetic  6.19 us (2%)
    all_gather x1, waiting for transfers between devices, per_device(): lax.all_gather(key_value_weight, 'seq', axis=0, tiled=True)  124 us
    psum x1, blocking collectives, per_device(): d_latent = lax.psum(local_grad, 'head').astype(jnp.bfloat16)  43.3 us
    reduce_scatter x1, waiting for transfers between devices, per_device(): lax.psum_scatter(grad_down, 'seq', scatter_dimension=0, tiled=True)  43.3 us
    psum x1, blocking collectives, per_device(): latent = lax.psum(partial_value, 'head').astype(jnp.bfloat16)  41.2 us
    psum x1, blocking collectives, per_device(): misfit, energy = lax.psum((misfit_local, energy_local), ('seq', 'head'))  39.8 us
    dot_general x1, matrix products, per_device(): jnp.dot(hidden, lax.all_gather(key_value_weight, 'seq', axis=0, tiled=Tru...  17.2 us
  transfers between devices with their start and end apart: 3, of which 2 were waited for; matrix products, arithmetic and copies ran while one was open for 1% of the time, Pallas kernels for 0%

commit v1 on v0

v1 whole, which is shorter than its diff:
```python
import functools
import math

import jax
import jax.numpy as jnp
from jax import lax
from jax.experimental import pallas as pl
from jax.experimental.pallas import tpu as pltpu
from jax.sharding import PartitionSpec as P

KEY_VALUE_HEADS = 8
HEAD_SIZE = 128
THETA = 500000.0
MESH = pl.DeviceIdType.MESH
BF16 = jnp.bfloat16
F32 = jnp.float32


def rotation(positions):
    half_dim = HEAD_SIZE // 2
    freqs = jnp.power(
        jnp.float32(THETA), -(jnp.arange(half_dim, dtype=jnp.float32) * 2.0 / HEAD_SIZE)
    )
    angle = positions.astype(jnp.float32)[:, None] * freqs[None, :]
    cosine = jnp.cos(angle)
    sine = jnp.sin(angle)
    return (
        jnp.concatenate([cosine, cosine], axis=-1),
        jnp.concatenate([-sine, sine], axis=-1),
    )


def gather_kernel(
    A, B, chunks, minor_first,
    hidden_ref, weight_ref, cos_ref, sin_ref, out_ref,
    hid, wbuf, acc, hid_sem, own_sem, send_sem, recv_sem,
):
    s, h = lax.axis_index("seq"), lax.axis_index("head")
    a, b = s // B, s % B
    depth = hid.shape[1] // (A * B)
    cols = weight_ref.shape[-1]
    load = pltpu.make_async_copy(hidden_ref, hid, hid_sem)
    load.start()
    own = pltpu.make_async_copy(weight_ref, wbuf.at[s], own_sem)
    own.start()

    barrier = pltpu.get_barrier_semaphore()
    ways = (
        (a + 1 < A, s + B),
        (a > 0, s - B),
        (b + 1 < B, s + 1),
        (b > 0, s - 1),
    )
    for there, peer in ways:
        @pl.when(there)
        def _():
            pl.semaphore_signal(barrier, inc=1, device_id=(peer, h), device_id_type=MESH)
    met = sum(there.astype(jnp.int32) for there, _ in ways)
    pl.semaphore_wait(barrier, met)

    def copy(way, peer, o, i):
        return pltpu.make_async_remote_copy(
            src_ref=wbuf.at[o, i],
            dst_ref=wbuf.at[o, i],
            send_sem=send_sem.at[way, o, i],
            recv_sem=recv_sem.at[o, i],
            device_id=(peer, h),
            device_id_type=MESH,
        )

    def forwards(da, db, o, i, act):
        first = i < minor_first
        conds = (
            (da >= 0) & (first | (db == 0)),
            (da <= 0) & (first | (db == 0)),
            (db >= 0) & (jnp.logical_not(first) | (da == 0)),
            (db <= 0) & (jnp.logical_not(first) | (da == 0)),
        )
        for way in range(4):
            @pl.when(ways[way][0] & conds[way])
            def _():
                act(copy(way, ways[way][1], o, i))

    def product(o):
        start = pl.multiple_of(o * depth, depth)
        w = wbuf[o].reshape(depth, cols)
        rows = 256
        def tile(m, c):
            r = pl.ds(pl.multiple_of(m * rows, rows), rows)
            acc[r, :] += jnp.dot(hid[r, pl.ds(start, depth)], w, preferred_element_type=F32)
            return c
        lax.fori_loop(0, hid.shape[0] // rows, tile, 0)

    own.wait()

    def issue(i, c):
        forwards(0, 0, s, i, lambda d: d.start())
        return c
    lax.fori_loop(0, chunks, issue, 0)
    acc[...] = jnp.zeros_like(acc)
    load.wait()
    product(s)

    def combos(u):
        for e in range(B):
            for eb in ((1, -1) if e else (1,)):
                for sa in (1, -1):
                    yield e * eb, u + 1 - e, sa

    def each(u, act):
        for off_b, d, sa in combos(u):
            a0, b0 = a + sa * d, b + off_b
            ok = (d >= 0) & (a0 >= 0) & (a0 < A) & (b0 >= 0) & (b0 < B)
            if sa < 0:
                ok = ok & (d > 0)

            @pl.when(ok)
            def _():
                act(a - a0, b - b0, a0 * B + b0)

    def stage(u, c):
        def chunk(i, c):
            def arrive(da, db, o):
                copy(0, s, o, i).wait_recv()
                forwards(da, db, o, i, lambda d: d.start())
            each(u, arrive)
            return c
        lax.fori_loop(0, chunks, chunk, 0)
        each(u, lambda da, db, o: product(o))
        return c
    lax.fori_loop(0, A + B - 2, stage, 0)

    def finish(o, c):
        def chunk(i, c):
            forwards(a - o // B, b - o % B, o, i, lambda d: d.wait_send())
            return c
        return lax.fori_loop(0, chunks, chunk, c)
    lax.fori_loop(0, A * B, finish, 0)

    for head in range(cols // (2 * HEAD_SIZE)):
        k0 = head * 2 * HEAD_SIZE
        key = acc[:, k0 : k0 + HEAD_SIZE]
        turned = key * cos_ref[...] + pltpu.roll(key, HEAD_SIZE // 2, 1) * sin_ref[...]
        out_ref[:, k0 : k0 + HEAD_SIZE] = turned.astype(BF16)
        out_ref[:, k0 + HEAD_SIZE : k0 + 2 * HEAD_SIZE] = acc[
            :, k0 + HEAD_SIZE : k0 + 2 * HEAD_SIZE
        ].astype(BF16)


def gather_targets(N, hidden, weight, cosine, sine):
    B = 2 if N <= 8 else 8
    A = N // B
    rows, width = hidden.shape
    depth, cols = weight.shape
    chunks = 8 if N <= 8 else 2
    minor_first = 1 if N <= 8 else 0
    shard = (chunks, depth // chunks, cols)
    return pl.pallas_call(
        functools.partial(gather_kernel, A, B, chunks, minor_first),
        out_shape=jax.ShapeDtypeStruct((rows, cols), BF16),
        in_specs=[pl.BlockSpec(memory_space=pl.ANY)] * 2
        + [pl.BlockSpec(memory_space=pltpu.VMEM)] * 2,
        out_specs=pl.BlockSpec(memory_space=pltpu.VMEM),
        scratch_shapes=[
            pltpu.VMEM((rows, width), BF16),
            pltpu.VMEM((N,) + shard, BF16),
            pltpu.VMEM((rows, cols), F32),
            pltpu.SemaphoreType.DMA,
            pltpu.SemaphoreType.DMA,
            pltpu.SemaphoreType.DMA((4, N, chunks)),
            pltpu.SemaphoreType.DMA((N, chunks)),
        ],
        compiler_params=pltpu.CompilerParams(
            collective_id=0, has_side_effects=True, vmem_limit_bytes=50 * 2**20
        ),
    )(hidden, weight.reshape(shard), cosine, sine)


def tail_kernel(
    N, H, entry_items, token_count,
    t_ref, d_ref, u_ref, gd_ref, gu_ref, rel_ref,
    snd, rcv, own, ybuf, lat, dlat, res, gsend, grecv, eh, es,
    c_send, c_recv, y_send, y_recv, g_send, g_recv, eh_send, eh_recv, es_send, es_recv,
):
    s, h = lax.axis_index("seq"), lax.axis_index("head")
    Y = H // 2
    y, core = h // 2, h % 2
    other = 1 - core
    sib = y * 2 + other
    chunks, _, half, cols = t_ref.shape
    rank = d_ref.shape[1]

    barrier = pltpu.get_barrier_semaphore()
    for j in range(1, H):
        pl.semaphore_signal(barrier, inc=1, device_id=(s, (h + j) % H), device_id_type=MESH)
    for j in range(1, N):
        pl.semaphore_signal(barrier, inc=1, device_id=((s + j) % N, h), device_id_type=MESH)

    def remote(src, dst, ssem, rsem, peer):
        return pltpu.make_async_remote_copy(
            src_ref=src, dst_ref=dst, send_sem=ssem, recv_sem=rsem,
            device_id=peer, device_id_type=MESH,
        )

    def to_sib(g, k):
        return remote(snd.at[g, k], rcv.at[g, k], c_send.at[g, 0, k], c_recv.at[g, 0, k], (s, sib))

    def back(g, k, slot):
        buf = lat if g == 0 else dlat
        return remote(buf.at[k, slot], buf.at[k, slot], c_send.at[g, 1, k], c_recv.at[g, 1, k], (s, sib))

    def to_y(g, k, slot, yy):
        return remote(
            ybuf.at[g, k, slot], ybuf.at[g, k, slot], y_send.at[g, k, yy], y_recv.at[g, k, slot],
            (s, yy * 2 + core),
        )

    def to_seq(g, slot, ss):
        return remote(gsend.at[g, ss], grecv.at[g, slot], g_send.at[g, ss], g_recv.at[g, slot], (ss, h))

    def nt(x, w):
        return lax.dot_general(x, w, (((1,), (1,)), ((), ())), preferred_element_type=F32)

    def tn(x, w):
        return lax.dot_general(x, w, (((0,), (0,)), ((), ())), preferred_element_type=F32)

    energy = jnp.zeros((), F32)
    for k in range(chunks):
        snd[0, k] = jnp.dot(t_ref[k, other], d_ref[...], preferred_element_type=F32).astype(BF16)
        if k == 0:
            pl.semaphore_wait(barrier, H - 1 + N - 1)
        to_sib(0, k).start()

    def meet(g, k):
        to_sib(g, k).wait_recv()
        ybuf[g, k, y] = (own[k] + rcv[g, k].astype(F32)).astype(BF16)
        for j in range(1, Y):
            to_y(g, k, y, (y + j) % Y).start()

    for k in range(chunks):
        own[k] = jnp.dot(t_ref[k, core], d_ref[...], preferred_element_type=F32)
        meet(0, k)
    for k in range(chunks):
        for c in range(2):
            wide = t_ref[k, c].astype(F32)
            energy += jnp.sum(wide * wide)

    def joined(g, k):
        for j in range(1, Y):
            to_y(g, k, (y + j) % Y, (y + j) % Y).wait_recv()
        total = ybuf[g, k, 0].astype(F32)
        for yy in range(1, Y):
            total += ybuf[g, k, yy].astype(F32)
        buf = lat if g == 0 else dlat
        buf[k, core] = total.astype(BF16)
        back(g, k, core).start()

    def residual(k, c):
        r = t_ref[k, c].astype(F32) - jnp.dot(lat[k, c], u_ref[...], preferred_element_type=F32)
        res[k, c] = r.astype(BF16)
        return jnp.sum(r * r)

    misfit = jnp.zeros((), F32)
    for k in range(chunks):
        joined(0, k)
    for k in range(chunks):
        back(0, k, other).wait_recv()
        misfit += residual(k, other)
        snd[1, k] = nt(res[k, other], u_ref[...]).astype(BF16)
        to_sib(1, k).start()
    for k in range(chunks):
        misfit += residual(k, core)
        own[k] = nt(res[k, core], u_ref[...])
        meet(1, k)

    tile = eh.shape[-2:]
    eh[h, 0] = jnp.full(tile, energy, F32)
    eh[h, 1] = jnp.full(tile, misfit, F32)

    def to_head(slot, hh):
        return remote(eh.at[slot], eh.at[slot], eh_send.at[hh], eh_recv.at[slot], (s, hh))

    def to_all(slot, ss):
        return remote(es.at[slot], es.at[slot], es_send.at[ss], es_recv.at[slot], (ss, h))

    for j in range(1, H):
        to_head(h, (h + j) % H).start()

    def scatter(g, left, right):
        grad = tn(left[...].reshape(-1, rank), right[...].reshape(-1, cols))
        gsend[g] = grad.reshape(gsend.shape[1:]).astype(BF16)
        for j in range(1, N):
            ss = (s + j) % N
            to_seq(g, s, ss).start()

    scatter(0, lat, res)
    for j in range(1, H):
        hh = (h + j) % H
        to_head(hh, hh).wait_recv()
    total = eh[0]
    for hh in range(1, H):
        total += eh[hh]
    es[s] = total
    for j in range(1, N):
        to_all(s, (s + j) % N).start()

    for k in range(chunks):
        joined(1, k)
    for k in range(chunks):
        back(1, k, other).wait_recv()
    scatter(1, dlat, t_ref)

    for j in range(1, N):
        ss = (s + j) % N
        to_all(ss, ss).wait_recv()
    total = es[0]
    for ss in range(1, N):
        total += es[ss]
    whole_energy, whole_misfit = total[0], total[1]
    rel_ref[...] = whole_misfit / whole_energy
    factor = (-(entry_items / whole_energy) / math.sqrt(token_count))[0:1, 0:1]

    for g, out in ((0, gu_ref), (1, gd_ref)):
        total = gsend[g, s].astype(F32)
        for j in range(1, N):
            ss = (s + j) % N
            to_seq(g, ss, ss).wait_recv()
            total += grecv[g, ss].astype(F32)
        out[...] = factor * total

    for g in range(2):
        for k in range(chunks):
            to_sib(g, k).wait_send()
            back(g, k, core).wait_send()
            for j in range(1, Y):
                to_y(g, k, y, (y + j) % Y).wait_send()
        for j in range(1, N):
            to_seq(g, s, (s + j) % N).wait_send()
    for j in range(1, H):
        to_head(h, (h + j) % H).wait_send()
    for j in range(1, N):
        to_all(s, (s + j) % N).wait_send()


def tail(N, H, targets, down, up):
    rows, cols = targets.shape
    rank = down.shape[1]
    chunks = 4
    half = rows // chunks // 2
    block = rank // N
    Y = H // 2
    dma = pltpu.SemaphoreType.DMA
    vmem = pl.BlockSpec(memory_space=pltpu.VMEM)
    token_count = N * rows
    return pl.pallas_call(
        functools.partial(
            tail_kernel, N, H, token_count * 2 * KEY_VALUE_HEADS * HEAD_SIZE, token_count
        ),
        out_shape=(
            jax.ShapeDtypeStruct((block, cols), F32),
            jax.ShapeDtypeStruct((block, cols), F32),
            jax.ShapeDtypeStruct((8, 128), F32),
        ),
        in_specs=[vmem] * 3,
        out_specs=(vmem,) * 3,
        scratch_shapes=[
            pltpu.VMEM((2, chunks, half, rank), BF16),
            pltpu.VMEM((2, chunks, half, rank), BF16),
            pltpu.VMEM((chunks, half, rank), F32),
            pltpu.VMEM((2, chunks, Y, half, rank), BF16),
            pltpu.VMEM((chunks, 2, half, rank), BF16),
            pltpu.VMEM((chunks, 2, half, rank), BF16),
            pltpu.VMEM((chunks, 2, half, cols), BF16),
            pltpu.VMEM((2, N, block, cols), BF16),
            pltpu.VMEM((2, N, block, cols), BF16),
            pltpu.VMEM((H, 2, 8, 128), F32),
            pltpu.VMEM((N, 2, 8, 128), F32),
            dma((2, 2, chunks)),
            dma((2, 2, chunks)),
            dma((2, chunks, Y)),
            dma((2, chunks, Y)),
            dma((2, N)),
            dma((2, N)),
            dma((H,)),
            dma((H,)),
            dma((N,)),
            dma((N,)),
        ],
        compiler_params=pltpu.CompilerParams(
            collective_id=1, has_side_effects=True, vmem_limit_bytes=48 * 2**20
        ),
    )(targets.reshape(chunks, 2, half, cols), down, up)


def solution(mesh):
    N, H = mesh.shape["seq"], mesh.shape["head"]

    def per_device(hidden, key_value_weight, down_projection, up_projection, positions):
        cosine, sine = rotation(positions)
        targets = gather_targets(N, hidden, key_value_weight, cosine, sine)
        grad_down, grad_up, rel = tail(N, H, targets, down_projection, up_projection)
        return grad_down, grad_up, rel[0, 0]

    return jax.shard_map(
        per_device,
        mesh=mesh,
        in_specs=(P("seq", None), P("seq", "head"), P("head", None), P(None, "head"), P("seq")),
        out_specs=(P("seq", "head"), P("seq", "head"), P()),
        check_vma=False,
    )
```

time: 350 us -> 150 us (0.43)
  waiting for transfers between devices: 168 us -> 0 us
  Pallas kernels: 0 us -> 142 us
  blocking collectives: 124 us -> 0 us
  matrix products: 30.4 us -> 0 us
  between operations: 17 us -> 0.7 us
    pallas_call x0 -> x2, Pallas kernels: none -> 142 us  [the longest x1 93.9 us: gather_targets(): pl.pallas_call(functools.partial(gather_kernel, A, B, chunks, minor_first...]
    all_gather x1 -> x0, waiting for transfers between devices: 124 us -> none  [per_device(): lax.all_gather(key_value_weight, 'seq', axis=0, tiled=True)]
    psum x3 -> x0, blocking collectives: 124 us -> none  [the longest x1 43.3 us: per_device(): d_latent = lax.psum(local_grad, 'head').astype(jnp.bfloat16)]
    reduce_scatter x2 -> x0, waiting for transfers between devices: 43.4 us -> none  [the longest x1 43.3 us: per_device(): lax.psum_scatter(grad_down, 'seq', scatter_dimension=0, tiled=True)]
    dot_general x6 -> x0, matrix products: 30.4 us -> none  [the longest x1 17.2 us: per_device(): jnp.dot(hidden, lax.all_gather(key_value_weight, 'seq', axis=0, tiled=Tru...]
  transfers between devices with their start and end apart: 3 -> 0, of which waited for: 2 -> 0; matrix products, arithmetic and copies ran while one was open for 1% -> 0% of each run, Pallas kernels for 0% -> 0%
where the time goes in v1:
time: 150 us; the launch traced here: 149 us
  Pallas kernels  142 us (95%)
  local copies, waits for them, and re-layouts  3.05 us (2%)
  other arithmetic  3.02 us (2%)
    pallas_call x1, Pallas kernels, gather_targets(): pl.pallas_call(functools.partial(gather_kernel, A, B, chunks, minor_first...  93.9 us
    pallas_call x1, Pallas kernels, tail(): pl.pallas_call(functools.partial(tail_kernel, N, H, token_count * 2 * KEY...  48.3 us

profile of v1, /device:TPU:8, one launch (start us, length us, event | category | flops | bytes accessed | tf_op | source)
XLA Modules:
  0.0 149.0 jit_solution(13755209502159714745)
XLA Ops:
  0.6 0.0 copy-start.2
  0.6 0.0 copy-start.1
  0.7 0.8 convert_element_type.3
  1.4 1.9 %fusion = (f32[1024,64]{1,0:T(8,128)S(1)}, f32[1024,64]{1,0:T(8,128)S(1)}, f32[1024,64]{1,0:T(8,128)S(1)}) fusion(f32[64]{0:T(128)S(1)} %negate_power_fusion, f32[1024]{0:T(1024)S(1)} %convert_element_type.3), kind=kLoop, calls=%fused_computation.4 | loop fusion | flops 131072 | bytes 790784 | tf_op jit(solution)/shard_map/neg | solution.py:29
  3.3 0.3 pad_maximum_fusion
  3.7 0.0 copy-start
  3.7 1.2 copy-done
  4.9 93.9 %shard_map.76 = bf16[1024,512]{1,0:T(8,128)(2,1)S(1)} custom-call(bf16[1024,8192]{1,0:T(8,128)(2,1)} %hidden_ref.1, bf16[8,128,512]{2,1,0:T(8,128)(2,1)S(1)} %bitcast.4, f32[1024,128]{1,0:T(8,128)S(1)} %get-tuple-element.12.cos_ref, f32[1024,128]{1,0:T(8,128)S(1)} %get-tuple-element.13.sin_ref), custom_call_target="tpu_custom_call" | custom-call | tf_op jit(solution)/shard_map/pallas_call | solution.py:158
  98.8 0.0 copy-done.2
  98.8 0.0 copy-done.1
  98.9 48.3 %shard_map.77 = (f32[64,512]{1,0:T(8,128)S(1)}, f32[64,512]{1,0:T(8,128)S(1)}, f32[8,128]{1,0:T(8,128)S(1)}) custom-call(bf16[4,2,128,512]{3,2,1,0:T(8,128)(2,1)S(1)} %bitcast.3, bf16[512,512]{1,0:T(8,128)(2,1)S(1)} %copy-done.1, bf16[512,512]{1,0:T(8,128)(2,1)S(1)} %copy-done.2), custom_call_target="tpu_custom_call" | custom-call | tf_op jit(solution)/shard_map/pallas_call | solution.py:355
  147.2 0.5 slice.3
  147.7 0.7 copy.10
  148.3 0.7 copy.11
  (1 shorter events, 0.0 us)
Async XLA Ops:
  0.6 98.2 %copy-start.2 = (bf16[512,512]{1,0:T(8,128)(2,1)S(1)}, bf16[512,512]{1,0:T(8,128)(2,1)}, u32[]{:S(2)}) copy-start(bf16[512,512]{1,0:T(8,128)(2,1)} %u_ref.1) | copy-start | bytes 1572868
  0.6 98.2 %copy-start.1 = (bf16[512,512]{1,0:T(8,128)(2,1)S(1)}, bf16[512,512]{1,0:T(8,128)(2,1)}, u32[]{:S(2)}) copy-start(bf16[512,512]{1,0:T(8,128)(2,1)} %d_ref.1) | copy-start | bytes 1572868
  3.7 1.2 copy-start

commit v2 on v1

--- a/solution.py
+++ b/solution.py
@@ -31,7 +31,7 @@
 
 
 def gather_kernel(
-    A, B, chunks, minor_first,
+    A, B, chunks, groups, minor_first,
     hidden_ref, weight_ref, cos_ref, sin_ref, out_ref,
     hid, wbuf, acc, hid_sem, own_sem, send_sem, recv_sem,
 ):
@@ -81,13 +81,16 @@
             def _():
                 act(copy(way, ways[way][1], o, i))
 
-    def product(o):
-        start = pl.multiple_of(o * depth, depth)
-        w = wbuf[o].reshape(depth, cols)
+    piece = depth // groups
+    span = chunks // groups
+
+    def product(o, q):
+        start = pl.multiple_of(o * depth + q * piece, piece)
+        w = wbuf[o, pl.ds(q * span, span)].reshape(piece, cols)
         rows = 256
         def tile(m, c):
             r = pl.ds(pl.multiple_of(m * rows, rows), rows)
-            acc[r, :] += jnp.dot(hid[r, pl.ds(start, depth)], w, preferred_element_type=F32)
+            acc[r, :] += jnp.dot(hid[r, pl.ds(start, piece)], w, preferred_element_type=F32)
             return c
         lax.fori_loop(0, hid.shape[0] // rows, tile, 0)
 
@@ -99,7 +102,11 @@
     lax.fori_loop(0, chunks, issue, 0)
     acc[...] = jnp.zeros_like(acc)
     load.wait()
-    product(s)
+
+    def own_product(q, c):
+        product(s, q)
+        return c
+    lax.fori_loop(0, groups, own_product, 0)
 
     def combos(u):
         for e in range(B):
@@ -119,15 +126,19 @@
                 act(a - a0, b - b0, a0 * B + b0)
 
     def stage(u, c):
-        def chunk(i, c):
-            def arrive(da, db, o):
-                copy(0, s, o, i).wait_recv()
-                forwards(da, db, o, i, lambda d: d.start())
-            each(u, arrive)
+        def group(q, c):
+            def chunk(j, c):
+                i = q * span + j
+
+                def arrive(da, db, o):
+                    copy(0, s, o, i).wait_recv()
+                    forwards(da, db, o, i, lambda d: d.start())
+                each(u, arrive)
+                return c
+            lax.fori_loop(0, span, chunk, 0)
+            each(u, lambda da, db, o: product(o, q))
             return c
-        lax.fori_loop(0, chunks, chunk, 0)
-        each(u, lambda da, db, o: product(o))
-        return c
+        return lax.fori_loop(0, groups, group, c)
     lax.fori_loop(0, A + B - 2, stage, 0)
 
     def finish(o, c):
@@ -152,11 +163,12 @@
     A = N // B
     rows, width = hidden.shape
     depth, cols = weight.shape
-    chunks = 8 if N <= 8 else 2
-    minor_first = 1 if N <= 8 else 0
+    chunks = 16 if N <= 8 else 2
+    groups = max(1, depth // 256)
+    minor_first = 3 if N <= 8 else 0
     shard = (chunks, depth // chunks, cols)
     return pl.pallas_call(
-        functools.partial(gather_kernel, A, B, chunks, minor_first),
+        functools.partial(gather_kernel, A, B, chunks, groups, minor_first),
         out_shape=jax.ShapeDtypeStruct((rows, cols), BF16),
         in_specs=[pl.BlockSpec(memory_space=pl.ANY)] * 2
         + [pl.BlockSpec(memory_space=pltpu.VMEM)] * 2,
@@ -179,7 +191,7 @@
 def tail_kernel(
     N, H, entry_items, token_count,
     t_ref, d_ref, u_ref, gd_ref, gu_ref, rel_ref,
-    snd, rcv, own, ybuf, lat, dlat, res, gsend, grecv, eh, es,
+    snd, rcv, own, gacc, ybuf, lat, dlat, res, gsend, grecv, eh, es,
     c_send, c_recv, y_send, y_recv, g_send, g_recv, eh_send, eh_recv, es_send, es_recv,
 ):
     s, h = lax.axis_index("seq"), lax.axis_index("head")
@@ -261,17 +273,21 @@
         return jnp.sum(r * r)
 
     misfit = jnp.zeros((), F32)
-    for k in range(chunks):
-        joined(0, k)
-    for k in range(chunks):
-        back(0, k, other).wait_recv()
-        misfit += residual(k, other)
-        snd[1, k] = nt(res[k, other], u_ref[...]).astype(BF16)
-        to_sib(1, k).start()
-    for k in range(chunks):
-        misfit += residual(k, core)
-        own[k] = nt(res[k, core], u_ref[...])
-        meet(1, k)
+    for step in range(chunks + 2):
+        k = step
+        if k < chunks:
+            joined(0, k)
+        k = step - 1
+        if 0 <= k < chunks:
+            back(0, k, other).wait_recv()
+            misfit += residual(k, other)
+            snd[1, k] = nt(res[k, other], u_ref[...]).astype(BF16)
+            to_sib(1, k).start()
+            misfit += residual(k, core)
+            own[k] = nt(res[k, core], u_ref[...])
+        k = step - 2
+        if 0 <= k < chunks:
+            meet(1, k)
 
     tile = eh.shape[-2:]
     eh[h, 0] = jnp.full(tile, energy, F32)
@@ -286,14 +302,13 @@
     for j in range(1, H):
         to_head(h, (h + j) % H).start()
 
-    def scatter(g, left, right):
-        grad = tn(left[...].reshape(-1, rank), right[...].reshape(-1, cols))
+    def scatter(g, grad):
         gsend[g] = grad.reshape(gsend.shape[1:]).astype(BF16)
         for j in range(1, N):
             ss = (s + j) % N
             to_seq(g, s, ss).start()
 
-    scatter(0, lat, res)
+    scatter(0, tn(lat[...].reshape(-1, rank), res[...].reshape(-1, cols)))
     for j in range(1, H):
         hh = (h + j) % H
         to_head(hh, hh).wait_recv()
@@ -304,11 +319,19 @@
     for j in range(1, N):
         to_all(s, (s + j) % N).start()
 
-    for k in range(chunks):
-        joined(1, k)
-    for k in range(chunks):
-        back(1, k, other).wait_recv()
-    scatter(1, dlat, t_ref)
+    for k in range(chunks + 1):
+        if k < chunks:
+            joined(1, k)
+        if k == 0:
+            continue
+        back(1, k - 1, other).wait_recv()
+        part = tn(dlat[k - 1].reshape(-1, rank), t_ref[k - 1].reshape(-1, cols))
+        if k == 1:
+            gacc[...] = part
+        elif k < chunks:
+            gacc[...] += part
+        else:
+            scatter(1, gacc[...] + part)
 
     for j in range(1, N):
         ss = (s + j) % N
@@ -367,6 +390,7 @@
             pltpu.VMEM((2, chunks, half, rank), BF16),
             pltpu.VMEM((2, chunks, half, rank), BF16),
             pltpu.VMEM((chunks, half, rank), F32),
+            pltpu.VMEM((rank, cols), F32),
             pltpu.VMEM((2, chunks, Y, half, rank), BF16),
             pltpu.VMEM((chunks, 2, half, rank), BF16),
             pltpu.VMEM((chunks, 2, half, rank), BF16),

time: 150 us -> 155 us (1.033)
  Pallas kernels: 142 us -> 147 us
    pallas_call x1, Pallas kernels: 48.3 us -> 51.7 us  [tail(): pl.pallas_call(functools.partial(tail_kernel, N, H, token_count * 2 * KEY...]
    pallas_call x1, Pallas kernels: 93.9 us -> 95.6 us  [gather_targets(): pl.pallas_call(functools.partial(gather_kernel, A, B, chunks, groups, min...]
where the time goes in v2:
time: 155 us; the launch traced here: 154 us
  Pallas kernels  147 us (95%)
  local copies, waits for them, and re-layouts  3.05 us (2%)
  other arithmetic  3.02 us (2%)
    pallas_call x1, Pallas kernels, gather_targets(): pl.pallas_call(functools.partial(gather_kernel, A, B, chunks, groups, min...  95.6 us
    pallas_call x1, Pallas kernels, tail(): pl.pallas_call(functools.partial(tail_kernel, N, H, token_count * 2 * KEY...  51.7 us

profile of v2, /device:TPU:8, one launch (start us, length us, event | category | flops | bytes accessed | tf_op | source)
XLA Modules:
  0.0 154.1 jit_solution(2363909133238279906)
XLA Ops:
  0.6 0.0 copy-start.2
  0.6 0.0 copy-start.1
  0.7 0.8 convert_element_type.3
  1.4 1.9 %fusion = (f32[1024,64]{1,0:T(8,128)S(1)}, f32[1024,64]{1,0:T(8,128)S(1)}, f32[1024,64]{1,0:T(8,128)S(1)}) fusion(f32[64]{0:T(128)S(1)} %negate_power_fusion, f32[1024]{0:T(1024)S(1)} %convert_element_type.3), kind=kLoop, calls=%fused_computation.4 | loop fusion | flops 131072 | bytes 790784 | tf_op jit(solution)/shard_map/neg | solution.py:29
  3.3 0.3 pad_maximum_fusion
  3.7 0.0 copy-start
  3.7 1.2 copy-done
  4.9 95.6 %shard_map.76 = bf16[1024,512]{1,0:T(8,128)(2,1)S(1)} custom-call(bf16[1024,8192]{1,0:T(8,128)(2,1)} %hidden_ref.1, bf16[16,64,512]{2,1,0:T(8,128)(2,1)S(1)} %bitcast.4, f32[1024,128]{1,0:T(8,128)S(1)} %get-tuple-element.12.cos_ref, f32[1024,128]{1,0:T(8,128)S(1)} %get-tuple-element.13.sin_ref), custom_call_target="tpu_custom_call" | custom-call | tf_op jit(solution)/shard_map/pallas_call | solution.py:170
  100.5 0.0 copy-done.2
  100.6 0.0 copy-done.1
  100.6 51.7 %shard_map.77 = (f32[64,512]{1,0:T(8,128)S(1)}, f32[64,512]{1,0:T(8,128)S(1)}, f32[8,128]{1,0:T(8,128)S(1)}) custom-call(bf16[4,2,128,512]{3,2,1,0:T(8,128)(2,1)S(1)} %bitcast.3, bf16[512,512]{1,0:T(8,128)(2,1)S(1)} %copy-done.1, bf16[512,512]{1,0:T(8,128)(2,1)S(1)} %copy-done.2), custom_call_target="tpu_custom_call" | custom-call | tf_op jit(solution)/shard_map/pallas_call | solution.py:378
  152.2 0.5 slice.3
  152.7 0.7 copy.10
  153.4 0.7 copy.11
  (1 shorter events, 0.0 us)
Async XLA Ops:
  0.6 99.9 %copy-start.2 = (bf16[512,512]{1,0:T(8,128)(2,1)S(1)}, bf16[512,512]{1,0:T(8,128)(2,1)}, u32[]{:S(2)}) copy-start(bf16[512,512]{1,0:T(8,128)(2,1)} %u_ref.1) | copy-start | bytes 1572868
  0.6 99.9 %copy-start.1 = (bf16[512,512]{1,0:T(8,128)(2,1)S(1)}, bf16[512,512]{1,0:T(8,128)(2,1)}, u32[]{:S(2)}) copy-start(bf16[512,512]{1,0:T(8,128)(2,1)} %d_ref.1) | copy-start | bytes 1572868
  3.7 1.2 copy-start

commit v3 on v2

--- a/solution.py
+++ b/solution.py
@@ -163,9 +163,9 @@
     A = N // B
     rows, width = hidden.shape
     depth, cols = weight.shape
-    chunks = 16 if N <= 8 else 2
+    chunks = 8 if N <= 8 else 2
     groups = max(1, depth // 256)
-    minor_first = 3 if N <= 8 else 0
+    minor_first = 1 if N <= 8 else 0
     shard = (chunks, depth // chunks, cols)
     return pl.pallas_call(
         functools.partial(gather_kernel, A, B, chunks, groups, minor_first),

time: 155 us -> 147 us (0.948)
  Pallas kernels: 147 us -> 140 us
    pallas_call x1, Pallas kernels: 51.7 us -> 47.1 us  [tail(): pl.pallas_call(functools.partial(tail_kernel, N, H, token_count * 2 * KEY...]
    pallas_call x1, Pallas kernels: 95.6 us -> 93.2 us  [gather_targets(): pl.pallas_call(functools.partial(gather_kernel, A, B, chunks, groups, min...]
where the time goes in v3:
time: 147 us
  Pallas kernels  140 us (95%)
  local copies, waits for them, and re-layouts  3.05 us (2%)
  other arithmetic  3.02 us (2%)
    pallas_call x1, Pallas kernels, gather_targets(): pl.pallas_call(functools.partial(gather_kernel, A, B, chunks, groups, min...  93.2 us
    pallas_call x1, Pallas kernels, tail(): pl.pallas_call(functools.partial(tail_kernel, N, H, token_count * 2 * KEY...  47.1 us

profile of v3, /device:TPU:8, one launch (start us, length us, event | category | flops | bytes accessed | tf_op | source)
XLA Modules:
  0.0 147.1 jit_solution(9443150883998164465)
XLA Ops:
  0.6 0.0 copy-start.2
  0.6 0.0 copy-start.1
  0.7 0.8 convert_element_type.3
  1.4 1.9 %fusion = (f32[1024,64]{1,0:T(8,128)S(1)}, f32[1024,64]{1,0:T(8,128)S(1)}, f32[1024,64]{1,0:T(8,128)S(1)}) fusion(f32[64]{0:T(128)S(1)} %negate_power_fusion, f32[1024]{0:T(1024)S(1)} %convert_element_type.3), kind=kLoop, calls=%fused_computation.4 | loop fusion | flops 131072 | bytes 790784 | tf_op jit(solution)/shard_map/neg | solution.py:29
  3.3 0.3 pad_maximum_fusion
  3.7 0.0 copy-start
  3.7 1.2 copy-done
  4.9 93.2 %shard_map.76 = bf16[1024,512]{1,0:T(8,128)(2,1)S(1)} custom-call(bf16[1024,8192]{1,0:T(8,128)(2,1)} %hidden_ref.1, bf16[8,128,512]{2,1,0:T(8,128)(2,1)S(1)} %bitcast.4, f32[1024,128]{1,0:T(8,128)S(1)} %get-tuple-element.12.cos_ref, f32[1024,128]{1,0:T(8,128)S(1)} %get-tuple-element.13.sin_ref), custom_call_target="tpu_custom_call" | custom-call | tf_op jit(solution)/shard_map/pallas_call | solution.py:170
  98.1 0.0 copy-done.2
  98.2 0.0 copy-done.1
  98.2 47.1 %shard_map.77 = (f32[64,512]{1,0:T(8,128)S(1)}, f32[64,512]{1,0:T(8,128)S(1)}, f32[8,128]{1,0:T(8,128)S(1)}) custom-call(bf16[4,2,128,512]{3,2,1,0:T(8,128)(2,1)S(1)} %bitcast.3, bf16[512,512]{1,0:T(8,128)(2,1)S(1)} %copy-done.1, bf16[512,512]{1,0:T(8,128)(2,1)S(1)} %copy-done.2), custom_call_target="tpu_custom_call" | custom-call | tf_op jit(solution)/shard_map/pallas_call | solution.py:378
  145.3 0.5 slice.3
  145.8 0.7 copy.10
  146.4 0.7 copy.11
  (1 shorter events, 0.0 us)
Async XLA Ops:
  0.6 97.5 %copy-start.2 = (bf16[512,512]{1,0:T(8,128)(2,1)S(1)}, bf16[512,512]{1,0:T(8,128)(2,1)}, u32[]{:S(2)}) copy-start(bf16[512,512]{1,0:T(8,128)(2,1)} %u_ref.1) | copy-start | bytes 1572868
  0.6 97.5 %copy-start.1 = (bf16[512,512]{1,0:T(8,128)(2,1)S(1)}, bf16[512,512]{1,0:T(8,128)(2,1)}, u32[]{:S(2)}) copy-start(bf16[512,512]{1,0:T(8,128)(2,1)} %d_ref.1) | copy-start | bytes 1572868
  3.7 1.2 copy-start

commit v4 on v3

--- a/solution.py
+++ b/solution.py
@@ -138,15 +138,16 @@
             lax.fori_loop(0, span, chunk, 0)
             each(u, lambda da, db, o: product(o, q))
             return c
-        return lax.fori_loop(0, groups, group, c)
+        lax.fori_loop(0, groups, group, 0)
+
+        def sent(da, db, o):
+            def chunk(i, c):
+                forwards(da, db, o, i, lambda d: d.wait_send())
+                return c
+            lax.fori_loop(0, chunks, chunk, 0)
+        each(u - 1, sent)
+        return c
     lax.fori_loop(0, A + B - 2, stage, 0)
-
-    def finish(o, c):
-        def chunk(i, c):
-            forwards(a - o // B, b - o % B, o, i, lambda d: d.wait_send())
-            return c
-        return lax.fori_loop(0, chunks, chunk, c)
-    lax.fori_loop(0, A * B, finish, 0)
 
     for head in range(cols // (2 * HEAD_SIZE)):
         k0 = head * 2 * HEAD_SIZE

time: 147 us -> 146 us (level)
  no operation moved by 1% of the time
where the time goes in v4:
time: 146 us
  Pallas kernels  140 us (96%)
  local copies, waits for them, and re-layouts  3.05 us (2%)
  other arithmetic  3.02 us (2%)
    pallas_call x1, Pallas kernels, gather_targets(): pl.pallas_call(functools.partial(gather_kernel, A, B, chunks, groups, min...  92.4 us
    pallas_call x1, Pallas kernels, tail(): pl.pallas_call(functools.partial(tail_kernel, N, H, token_count * 2 * KEY...  47.1 us

profile of v4, /device:TPU:8, one launch (start us, length us, event | category | flops | bytes accessed | tf_op | source)
XLA Modules:
  0.0 146.3 jit_solution(10876795067384305086)
XLA Ops:
  0.6 0.0 copy-start.2
  0.6 0.0 copy-start.1
  0.7 0.8 convert_element_type.3
  1.4 1.9 %fusion = (f32[1024,64]{1,0:T(8,128)S(1)}, f32[1024,64]{1,0:T(8,128)S(1)}, f32[1024,64]{1,0:T(8,128)S(1)}) fusion(f32[64]{0:T(128)S(1)} %negate_power_fusion, f32[1024]{0:T(1024)S(1)} %convert_element_type.3), kind=kLoop, calls=%fused_computation.4 | loop fusion | flops 131072 | bytes 790784 | tf_op jit(solution)/shard_map/neg | solution.py:29
  3.3 0.3 pad_maximum_fusion
  3.7 0.0 copy-start
  3.7 1.2 copy-done
  4.9 92.4 %shard_map.76 = bf16[1024,512]{1,0:T(8,128)(2,1)S(1)} custom-call(bf16[1024,8192]{1,0:T(8,128)(2,1)} %hidden_ref.1, bf16[8,128,512]{2,1,0:T(8,128)(2,1)S(1)} %bitcast.4, f32[1024,128]{1,0:T(8,128)S(1)} %get-tuple-element.12.cos_ref, f32[1024,128]{1,0:T(8,128)S(1)} %get-tuple-element.13.sin_ref), custom_call_target="tpu_custom_call" | custom-call | tf_op jit(solution)/shard_map/pallas_call | solution.py:171
  97.4 0.0 copy-done.2
  97.4 0.0 copy-done.1
  97.4 47.1 %shard_map.77 = (f32[64,512]{1,0:T(8,128)S(1)}, f32[64,512]{1,0:T(8,128)S(1)}, f32[8,128]{1,0:T(8,128)S(1)}) custom-call(bf16[4,2,128,512]{3,2,1,0:T(8,128)(2,1)S(1)} %bitcast.3, bf16[512,512]{1,0:T(8,128)(2,1)S(1)} %copy-done.1, bf16[512,512]{1,0:T(8,128)(2,1)S(1)} %copy-done.2), custom_call_target="tpu_custom_call" | custom-call | tf_op jit(solution)/shard_map/pallas_call | solution.py:379
  144.5 0.5 slice.3
  145.0 0.7 copy.10
  145.6 0.7 copy.11
  (1 shorter events, 0.0 us)
Async XLA Ops:
  0.6 96.7 %copy-start.2 = (bf16[512,512]{1,0:T(8,128)(2,1)S(1)}, bf16[512,512]{1,0:T(8,128)(2,1)}, u32[]{:S(2)}) copy-start(bf16[512,512]{1,0:T(8,128)(2,1)} %u_ref.1) | copy-start | bytes 1572868
  0.6 96.7 %copy-start.1 = (bf16[512,512]{1,0:T(8,128)(2,1)S(1)}, bf16[512,512]{1,0:T(8,128)(2,1)}, u32[]{:S(2)}) copy-start(bf16[512,512]{1,0:T(8,128)(2,1)} %d_ref.1) | copy-start | bytes 1572868
  3.7 1.2 copy-start
